TPU v7x, 32 devices: a whole 2x2x4 slice. The times are simulated.
32 devices in a mesh: layer: 4 (over y, x), lat: 8 (over z, core).
Axes of the slice: x: 2, y: 2, z: 4, core: 2. Of those that a mesh axis runs over, the one named last changes fastest.
Arguments:
- activations: bfloat16 [8, 512, 2048], P(None, None, 'layer'), may hold values from -6 to 6
- targets: bfloat16 [8, 512, 2048], P(None, None, 'layer'), may hold values from -6 to 6
- encoder: bfloat16 [8, 2048, 8192], P(None, 'layer', 'lat'), may hold values from -0.125 to 0.125
- bias: float32 [8, 8192], P(None, 'lat'), may hold values from -3 to 3
- decoder: bfloat16 [36, 8192, 2048], P(None, 'lat', 'layer'), may hold values from -0.75 to 0.75
- active: int32 [8, 512, 64], replicated, may hold values from 0 to 8191, all different within a row
Outputs:
- grad_encoder: bfloat16 [8, 2048, 8192], P(None, 'layer', 'lat')
- grad_bias: float32 [8, 8192], P(None, 'lat')
- grad_decoder: bfloat16 [36, 8192, 2048], P(None, 'lat', 'layer')
Inputs may be any that keep to these rules, and one draw needn't show every extreme that they name: `active`: each row names 64 different latents.
All inputs are finite; a program needn't handle non-finite values.
Results may differ from a plain program's by a relative error of at most 0.0064.
Values may be sent and summed in bfloat16 or wider, within the bound.
A program may use at most 256 MiB of HBM per device.

v0:
```python
import jax
import jax.numpy as jnp
from jax import lax
from jax.sharding import PartitionSpec as P

LAYERS = 8


def pair_index(source, target):
    return source * LAYERS - source * (source - 1) // 2 + (target - source)


def on_device(activations, targets, encoder, bias, decoder, active):
    tokens = activations.shape[1]
    lat_width = encoder.shape[2]
    first = lax.axis_index("lat") * lat_width
    columns = first + jnp.arange(lat_width, dtype=jnp.int32)
    masks = jnp.stack(
        [
            jnp.any(active[source][:, :, None] == columns[None, None, :], axis=1)
            for source in range(LAYERS)
        ]
    ).astype(jnp.float32)
    partial_value = jnp.einsum(
        "ltd,ldf->ltf", activations, encoder, preferred_element_type=jnp.float32
    )
    preact = lax.psum(partial_value, "layer") + bias[:, None, :]
    latent_act = (preact * masks).astype(jnp.bfloat16)
    rebuilt_list = []
    for target in range(LAYERS):
        summed = jnp.dot(
            latent_act[0], decoder[pair_index(0, target)], preferred_element_type=jnp.float32
        )
        for source in range(1, target + 1):
            summed = summed + jnp.dot(
                latent_act[source],
                decoder[pair_index(source, target)],
                preferred_element_type=jnp.float32,
            )
        rebuilt_list.append(summed)
    rebuilt = jnp.stack(rebuilt_list)
    complete = lax.psum(rebuilt, "lat")
    errors = (complete - targets.astype(jnp.float32)).astype(jnp.bfloat16)
    by_tokens = (((0,), (0,)), ((), ()))
    by_width = (((1,), (1,)), ((), ()))
    grad_pairs = []
    for source in range(LAYERS):
        for target in range(source, LAYERS):
            grad_pairs.append(
                lax.dot_general(
                    latent_act[source],
                    errors[target],
                    by_tokens,
                    preferred_element_type=jnp.float32,
                ).astype(jnp.bfloat16)
            )
    grad_decoder = jnp.stack(grad_pairs)
    grad_list = []
    for source in range(LAYERS):
        summed = lax.dot_general(
            errors[source],
            decoder[pair_index(source, source)],
            by_width,
            preferred_element_type=jnp.float32,
        )
        for target in range(source + 1, LAYERS):
            summed = summed + lax.dot_general(
                errors[target],
                decoder[pair_index(source, target)],
                by_width,
                preferred_element_type=jnp.float32,
            )
        grad_list.append(summed)
    grad_partial = jnp.stack(grad_list)
    block_rows = tokens // lax.axis_size("layer")
    share_rows = lax.psum_scatter(grad_partial, "layer", scatter_dimension=1, tiled=True)
    mask_rows = lax.dynamic_slice_in_dim(masks, lax.axis_index("layer") * block_rows, block_rows, 1)
    grad_pre = lax.all_gather(
        (share_rows * mask_rows).astype(jnp.bfloat16), "layer", axis=1, tiled=True
    )
    grad_encoder = jnp.einsum(
        "ltd,ltf->ldf", activations, grad_pre, preferred_element_type=jnp.float32
    ).astype(jnp.bfloat16)
    grad_bias = jnp.sum(grad_pre.astype(jnp.float32), axis=1)
    return (grad_encoder, grad_bias, grad_decoder)


def solution(mesh):
    placed = (
        P(None, None, "layer"),
        P(None, None, "layer"),
        P(None, "layer", "lat"),
        P(None, "lat"),
        P(None, "lat", "layer"),
        P(),
    )
    return jax.shard_map(
        on_device,
        mesh=mesh,
        in_specs=placed,
        out_specs=(P(None, "layer", "lat"), P(None, "lat"), P(None, "lat", "layer")),
        check_vma=False,
    )
```

profile of v0, /device:TPU:0, one launch (start us, length us, event | category | flops | bytes accessed | tf_op | source)
XLA Modules:
  0.0 1017.3 jit_solution(10485353639587241992)
XLA Ops:
  7.2 15.4 %fusion.266 = f32[8,512,1024]{2,1,0:T(8,128)} fusion(bf16[8,512,512]{2,1,0:T(8,128)(2,1)} %param.6, bf16[8,512,1024]{2,1,0:T(8,128)(2,1)} %param.8), kind=kOutput, calls=%fused_computation.385 | convolution fusion | flops 4294967296 | bytes 29360128 | tf_op jit(solution)/shard_map/ltd,ldf->ltf/dot_general | solution.py:24
  25.0 192.2 %compare_reduce_fusion = (pred[512,1024]{1,0:T(8,128)(4,1)S(1)}, pred[512,1024]{1,0:T(8,128)(4,1)S(1)}, pred[512,1024]{1,0:T(8,128)(4,1)S(1)}, pred[512,1024]{1,...) fusion(s32[512,64]{1,0:T(8,128)S(1)} %copy.26, ...), kind=kLoop, calls=%fused_computation | loop fusion | flops 532676608 | bytes 5246976 | tf_op jit(solution)/shard_map/reduce_or | solution.py:20
  223.9 108.9 %all-reduce.3.cloned.1.call-done = f32[8,512,1024]{2,1,0:T(8,128)} async-done(((f32[8,512,1024]{2,1,0:T(8,128)}), f32[8,512,1024]{2,1,0:T(8,128)}) %all-reduce.3.cloned.1.call-update) | async-done | bytes 16777232 | tf_op jit(solution)/shard_map/psum | solution.py:27
  332.8 9.7 select_convert_fusion
  342.5 5.7 fusion.102
  348.3 2.0 fusion.124
  350.3 3.0 fusion.143
  353.4 3.0 fusion.159
  356.4 2.1 fusion.172
  360.4 3.1 fusion.14
  363.5 2.9 fusion.189
  366.4 3.1 convolution_add_fusion.6
  369.4 2.2 convolution_add_fusion.5
  384.4 2.9 convolution_add_fusion.9
  389.3 2.9 convolution_add_fusion.17
  392.2 2.9 convolution_add_fusion.16
  395.1 2.9 convolution_add_fusion.15
  398.0 2.9 convolution_add_fusion.14
  400.9 3.0 convolution_add_fusion.21
  403.9 3.0 convolution_add_fusion.20
  406.9 3.0 convolution_add_fusion.19
  409.9 13.2 %convolution_add_fusion.24 = f32[512,512]{1,0:T(8,128)} fusion(f32[512,512]{1,0:T(8,128)S(1)} %fusion.172, bf16[36,1024,512]{2,1,0:T(8,128)(2,1)S(1)} %bitcast.587, bf16[8,512,1024]{2,1,0:T(8,128)(2,1)S(1)} %select_convert_fusion), kind=kOutput, calls=%fused_computation.99 | convolution fusion | flops 537133056 | bytes 4194304 | tf_op jit(solution)/shard_map/dot_general | solution.py:35
  423.0 2.9 convolution_add_fusion.23
  427.7 3.0 fusion.13
  430.7 2.9 fusion.11
  433.6 2.9 fusion.9
  443.3 176.7 %all-reduce.5.cloned.1.call-done = f32[8,512,512]{2,1,0:T(8,128)} async-done(((f32[8,512,512]{2,1,0:T(8,128)}), f32[8,512,512]{2,1,0:T(8,128)}) %all-reduce.5.cloned.1.call-update) | async-done | bytes 8388624 | tf_op jit(solution)/shard_map/psum | solution.py:42
  619.9 6.0 subtract_convert_fusion
  626.0 2.7 fusion.122
  628.8 2.0 fusion.141
  636.6 3.3 fusion.187
  639.9 3.3 fusion.191
  643.3 3.3 fusion.119
  646.6 3.3 fusion.138
  649.8 3.3 fusion.154
  653.1 3.3 fusion.167
  656.4 3.3 fusion.177
  659.7 3.3 fusion.184
  672.9 3.3 fusion.113
  676.2 3.3 fusion.132
  679.5 3.3 fusion.148
  682.8 3.7 fusion.161
  692.4 3.3 fusion.107
  695.7 3.3 fusion.126
  699.0 3.3 fusion.104
  702.3 5.1 bitcast_dynamic-update-slice_fusion.7
  707.4 7.2 bitcast_dynamic-update-slice_fusion.6
  714.7 3.7 bitcast_dynamic-update-slice_fusion.5
  719.2 3.7 bitcast_dynamic-update-slice_fusion.4
  723.0 3.5 bitcast_dynamic-update-slice_fusion.3
  726.5 3.3 bitcast_dynamic-update-slice_fusion.2
  729.8 3.3 bitcast_dynamic-update-slice_fusion.1
  733.1 3.3 bitcast_dynamic-update-slice_fusion
  736.6 153.8 %reduce-scatter.2.cloned.1.call-done = f32[8,128,1024]{2,1,0:T(8,128)} async-done(((f32[8,512,1024]{2,1,0:T(8,128)}), f32[8,128,1024]{2,1,0:T(8,128)}) %reduce-scatter.2.cloned.1.call-update) | async-done | bytes 4194320 | tf_op jit(solution)/shard_map/reduce_scatter | solution.py:76
  890.4 4.6 multiply_convert_fusion
  895.0 3.2 fusion.16
  898.2 3.2 fusion.18
  901.4 3.1 fusion.20
  904.5 3.1 fusion.22
  907.7 2.9 fusion.24
  964.1 18.5 %all-gather.2.cloned.1.call-done = bf16[8,512,1024]{2,1,0:T(8,128)(2,1)} async-done(((bf16[8,128,1024]{2,1,0:T(8,128)(2,1)}), bf16[8,512,1024]{2,1,0:T(8,128)(2,1)}) %all-gather.2.cloned.1.call-update) | async-done | bytes 8388624 | tf_op jit(solution)/shard_map/all_gather | solution.py:78
  982.6 10.5 %convert_bitcast_fusion = bf16[8,512,1024]{1,2,0:T(8,128)(2,1)} fusion(bf16[8,512,1024]{2,1,0:T(8,128)(2,1)} %all-gather.2.cloned.1.call-done, bf16[8,512,512]{2,1,0:T(8,128)(2,1)} %param.6), kind=kOutput, calls=%fused_computation.10 | convolution fusion | flops 4299161600 | bytes 20971520 | tf_op jit(solution)/shard_map/ltd,ltf->ldf/dot_general | solution.py:81
  993.1 11.4 %copy.28 = bf16[8,512,1024]{2,1,0:T(8,128)(2,1)} copy(bf16[8,512,1024]{1,2,0:T(8,128)(2,1)} %convert_bitcast_fusion) | data formatting | bytes 16777216
  1004.4 5.9 convert_reduce_fusion
  (134 shorter events, 110.2 us)
Async XLA Ops:
  7.2 325.6 %all-reduce.3.cloned.1.call-start = ((), (), s32[]{:S(2)}) async-start(), calls=%async_computation.1 | async-start | bytes 33554432 | tf_op jit(solution)/shard_map/psum | solution.py:27
  22.6 1.2 copy-start.10
  22.6 597.4 %all-reduce.5.cloned.1.call-start = ((), (), s32[]{:S(2)}) async-start(), calls=%async_computation.2 | async-start | bytes 16777216 | tf_op jit(solution)/shard_map/psum | solution.py:42
  24.3 308.5 %copy-start.11 = (f32[8,1024]{1,0:T(8,128)S(1)}, f32[8,1024]{1,0:T(8,128)}, u32[]{:S(2)}) copy-start(f32[8,1024]{1,0:T(8,128)} %param.9) | copy-start | bytes 98308
  332.8 38.9 %slice-start = ((s8[37748736]{0:T(1024)(128)(4,1)}), s8[4194304]{0:T(1024)(128)(4,1)S(1)}, s32[]{:S(2)}) async-start(s8[37748736]{0:T(1024)(128)(4,1)} %bitcast.586), calls=%async_computation.5 | async-start | bytes 8388608
  332.8 38.9 %slice-start.1 = ((s8[37748736]{0:T(1024)(128)(4,1)}), s8[4194304]{0:T(1024)(128)(4,1)S(1)}, s32[]{:S(2)}) async-start(s8[37748736]{0:T(1024)(128)(4,1)} %bitcast.586), calls=%async_computation.6 | async-start | bytes 8388608
  332.8 38.9 %slice-start.2 = ((s8[37748736]{0:T(1024)(128)(4,1)}), s8[4194304]{0:T(1024)(128)(4,1)S(1)}, s32[]{:S(2)}) async-start(s8[37748736]{0:T(1024)(128)(4,1)} %bitcast.586), calls=%async_computation.7 | async-start | bytes 8388608
  332.8 38.9 %slice-start.3 = ((s8[37748736]{0:T(1024)(128)(4,1)}), s8[4194304]{0:T(1024)(128)(4,1)S(1)}, s32[]{:S(2)}) async-start(s8[37748736]{0:T(1024)(128)(4,1)} %bitcast.586), calls=%async_computation.8 | async-start | bytes 8388608
  342.5 99.0 %copy-start.9 = (bf16[8,512,1024]{2,1,0:T(8,128)(2,1)}, bf16[8,512,1024]{2,1,0:T(8,128)(2,1)S(1)}, u32[]{:S(2)}) copy-start(bf16[8,512,1024]{2,1,0:T(8,128)(2,1)S(1)} %select_convert_fusion) | copy-start | bytes 25165828
  342.5 29.2 %slice-start.4 = ((s8[37748736]{0:T(1024)(128)(4,1)}), s8[4194304]{0:T(1024)(128)(4,1)S(1)}, s32[]{:S(2)}) async-start(s8[37748736]{0:T(1024)(128)(4,1)} %bitcast.586), calls=%async_computation.9 | async-start | bytes 8388608
  350.3 21.4 %slice-start.5 = ((s8[37748736]{0:T(1024)(128)(4,1)}), s8[4194304]{0:T(1024)(128)(4,1)S(1)}, s32[]{:S(2)}) async-start(s8[37748736]{0:T(1024)(128)(4,1)} %bitcast.586), calls=%async_computation.10 | async-start | bytes 8388608
  356.4 15.4 %slice-start.6 = ((s8[37748736]{0:T(1024)(128)(4,1)}), s8[4194304]{0:T(1024)(128)(4,1)S(1)}, s32[]{:S(2)}) async-start(s8[37748736]{0:T(1024)(128)(4,1)} %bitcast.586), calls=%async_computation.11 | async-start | bytes 8388608
  360.4 11.4 %slice-start.7 = ((s8[37748736]{0:T(1024)(128)(4,1)}), s8[4194304]{0:T(1024)(128)(4,1)S(1)}, s32[]{:S(2)}) async-start(s8[37748736]{0:T(1024)(128)(4,1)} %bitcast.586), calls=%async_computation.12 | async-start | bytes 8388608
  366.4 5.4 slice-start.8
  426.0 10.5 %copy-start.13 = (f32[512,512]{1,0:T(8,128)S(1)}, f32[512,512]{1,0:T(8,128)}, u32[]{:S(2)}) copy-start(f32[512,512]{1,0:T(8,128)} %convolution_add_fusion.19) | copy-start | bytes 3145732
  427.7 10.5 %copy-start.12 = (f32[512,512]{1,0:T(8,128)S(1)}, f32[512,512]{1,0:T(8,128)}, u32[]{:S(2)}) copy-start(f32[512,512]{1,0:T(8,128)} %convolution_add_fusion.14) | copy-start | bytes 3145732
  443.2 447.2 %reduce-scatter.2.cloned.1.call-start = ((), (), s32[]{:S(2)}) async-start(), calls=%async_computation.3 | async-start | bytes 20971520 | tf_op jit(solution)/shard_map/reduce_scatter | solution.py:76
  626.0 107.1 %copy-start = (bf16[8,512,512]{2,1,0:T(8,128)(2,1)}, bf16[8,512,512]{2,1,0:T(8,128)(2,1)S(1)}, u32[]{:S(2)}) copy-start(bf16[8,512,512]{2,1,0:T(8,128)(2,1)S(1)} %subtract_convert_fusion) | copy-start | bytes 12582916
  714.7 3.7 copy-start.5
  714.7 3.7 copy-start.6
  714.7 3.7 copy-start.7
  714.7 4.5 copy-start.8
  719.2 7.2 copy-start.3
  719.2 7.2 copy-start.4
  723.0 6.8 copy-start.2
  736.4 246.2 %all-gather.2.cloned.1.call-start = ((), (), s32[]{:S(2)}) async-start(), calls=%async_computation.4 | async-start | bytes 10485760 | tf_op jit(solution)/shard_map/all_gather | solution.py:78
  895.0 6.5 copy-start.1
  898.2 12.4 %slice-start.9 = ((s8[8388608]{0:T(1024)(128)(4,1)}), s8[4194304]{0:T(1024)(128)(4,1)S(1)}, s32[]{:S(2)}) async-start(s8[8388608]{0:T(1024)(128)(4,1)} %bitcast.588), calls=%async_computation.14 | async-start | bytes 8388608
  904.5 6.1 slice-start.10
Sparse Core Ops, SparseCore 0:
  22.7 310.0 all-reduce.2
  443.3 176.5 all-reduce.4
  736.5 153.8 reduce-scatter.1
  895.1 87.4 all-gather.1
where the time goes:
time: 1030 us; the launch traced here: 1020 us
  waiting for transfers between devices  458 us (44%)
  matrix products  305 us (30%)
  other arithmetic  218 us (21%)
  local copies, waits for them, and re-layouts  21.2 us (2%)
  between operations  14.7 us (1%)
    reduce_or x1, other arithmetic, on_device(): jnp.any(active[source][:, :, None] == columns[None, None, :], axis=1)  192 us
    psum x1, waiting for transfers between devices, on_device(): complete = lax.psum(rebuilt, 'lat')  177 us
    reduce_scatter x1, waiting for transfers between devices, on_device(): lax.psum_scatter(grad_partial, 'layer', scatter_dimension=1, tiled=True)  154 us
    psum x1, waiting for transfers between devices, on_device(): preact = lax.psum(partial_value, 'layer') + bias[:, None, :]  109 us
    dot_general x28, matrix products, on_device(): lax.dot_general(errors[target], decoder[pair_index(source, target)], by_w...  85.2 us
    dot_general x28, matrix products, on_device(): jnp.dot(latent_act[source], decoder[pair_index(source, target)], preferre...  76.7 us
    dot_general x36, matrix products, on_device(): lax.dot_general(latent_act[source], errors[target], by_tokens, preferred_...  69.1 us
    dot_general x8, matrix products, on_device(): lax.dot_general(errors[source], decoder[pair_index(source, source)], by_w...  24.2 us
  transfers between devices with their start and end apart: 4, of which 4 were waited for; matrix products, arithmetic and copies ran while one was open for 26% of the time, Pallas kernels for 0%

commit v1 on v0

--- a/solution.py
+++ b/solution.py
@@ -4,6 +4,18 @@
 from jax.sharding import PartitionSpec as P
 
 LAYERS = 8
+
+
+def replace_circles(slab_in, axis_name):
+    fan = lax.axis_size(axis_name)
+    long_array, kept_arr = (slab_in, 0)
+    while 1 << kept_arr < fan:
+        mixed_arr = lax.ppermute(
+            long_array, axis_name, tuple(((idx, idx ^ 1 << kept_arr) for idx in range(fan)))
+        )
+        long_array = long_array + mixed_arr
+        kept_arr = kept_arr + 1
+    return long_array
 
 
 def pair_index(source, target):
@@ -39,7 +51,7 @@
             )
         rebuilt_list.append(summed)
     rebuilt = jnp.stack(rebuilt_list)
-    complete = lax.psum(rebuilt, "lat")
+    complete = replace_circles(rebuilt, "lat")
     errors = (complete - targets.astype(jnp.float32)).astype(jnp.bfloat16)
     by_tokens = (((0,), (0,)), ((), ()))
     by_width = (((1,), (1,)), ((), ()))

time: 1030 us -> 1440 us (1.40)
  waiting for transfers between devices: 458 us -> 837 us
  other arithmetic: 218 us -> 246 us
    ppermute x0 -> x3, waiting for transfers between devices: none -> 555 us  [replace_circles(): lax.ppermute(long_array, axis_name, tuple(((idx, idx ^ 1 << kept_arr) for...]
    psum x1 -> x0, waiting for transfers between devices: 177 us -> none  [on_device(): complete = lax.psum(rebuilt, 'lat')]
    add x0 -> x2, other arithmetic: none -> 22.5 us  [replace_circles(): long_array = long_array + mixed_arr]
  transfers between devices with their start and end apart: 4 -> 6, of which waited for: 4 -> 6; matrix products, arithmetic and copies ran while one was open for 26% -> 19% of each run, Pallas kernels for 0% -> 0%
where the time goes in v1:
time: 1440 us; the launch traced here: 1430 us
  waiting for transfers between devices  837 us (58%)
  matrix products  303 us (21%)
  other arithmetic  246 us (17%)
  local copies, waits for them, and re-layouts  24.7 us (2%)
  between operations  14.7 us (1%)
    ppermute x3, waiting for transfers between devices, replace_circles(): lax.ppermute(long_array, axis_name, tuple(((idx, idx ^ 1 << kept_arr) for...  555 us
    reduce_or x1, other arithmetic, on_device(): jnp.any(active[source][:, :, None] == columns[None, None, :], axis=1)  192 us
    reduce_scatter x1, waiting for transfers between devices, on_device(): lax.psum_scatter(grad_partial, 'layer', scatter_dimension=1, tiled=True)  155 us
    psum x1, waiting for transfers between devices, on_device(): preact = lax.psum(partial_value, 'layer') + bias[:, None, :]  109 us
    dot_general x28, matrix products, on_device(): lax.dot_general(errors[target], decoder[pair_index(source, target)], by_w...  83.9 us
    dot_general x28, matrix products, on_device(): jnp.dot(latent_act[source], decoder[pair_index(source, target)], preferre...  76.5 us
    dot_general x36, matrix products, on_device(): lax.dot_general(latent_act[source], errors[target], by_tokens, preferred_...  69.1 us
  transfers between devices with their start and end apart: 6, of which 6 were waited for; matrix products, arithmetic and copies ran while one was open for 19% of the time, Pallas kernels for 0%

profile of v1, /device:TPU:0, one launch (start us, length us, event | category | flops | bytes accessed | tf_op | source)
XLA Modules:
  0.0 1429.4 jit_solution(8310707014659480301)
XLA Ops:
  7.2 15.4 %fusion.266 = f32[8,512,1024]{2,1,0:T(8,128)} fusion(bf16[8,512,512]{2,1,0:T(8,128)(2,1)} %param.6, bf16[8,512,1024]{2,1,0:T(8,128)(2,1)} %param.8), kind=kOutput, calls=%fused_computation.385 | convolution fusion | flops 4294967296 | bytes 29360128 | tf_op jit(solution)/shard_map/ltd,ldf->ltf/dot_general | solution.py:36
  25.0 192.2 %compare_reduce_fusion = (pred[512,1024]{1,0:T(8,128)(4,1)S(1)}, pred[512,1024]{1,0:T(8,128)(4,1)S(1)}, pred[512,1024]{1,0:T(8,128)(4,1)S(1)}, pred[512,1024]{1,...) fusion(s32[512,64]{1,0:T(8,128)S(1)} %copy.26, ...), kind=kLoop, calls=%fused_computation | loop fusion | flops 532676608 | bytes 5246976 | tf_op jit(solution)/shard_map/reduce_or | solution.py:32
  223.9 108.9 %all-reduce.2.cloned.1.call-done = f32[8,512,1024]{2,1,0:T(8,128)} async-done(((f32[8,512,1024]{2,1,0:T(8,128)}), f32[8,512,1024]{2,1,0:T(8,128)}) %all-reduce.2.cloned.1.call-update) | async-done | bytes 16777232 | tf_op jit(solution)/shard_map/psum | solution.py:39
  332.8 9.6 select_convert_fusion
  342.5 5.7 fusion.103
  350.3 3.1 fusion.143
  353.4 2.9 fusion.159
  362.8 3.2 fusion.189
  366.0 3.4 convolution_add_fusion.6
  372.0 2.9 convolution_add_fusion.4
  377.2 2.9 convolution_add_fusion.2
  382.4 2.9 convolution_add_fusion.12
  387.5 2.9 convolution_add_fusion.10
  390.4 3.2 convolution_add_fusion.9
  395.9 3.3 convolution_add_fusion.17
  399.2 3.2 convolution_add_fusion.16
  402.4 3.2 convolution_add_fusion.15
  405.7 3.2 convolution_add_fusion.14
  408.9 3.2 convolution_add_fusion.21
  412.1 3.2 convolution_add_fusion.20
  415.4 3.2 convolution_add_fusion.19
  418.6 3.2 convolution_add_fusion.24
  421.8 3.3 convolution_add_fusion.23
  425.0 3.0 convolution_add_fusion.26
  442.7 3.4 copy-done.2
  446.1 13.3 collective-permute-done
  459.4 11.3 add.234
  472.1 181.3 %collective-permute-done.1 = f32[8,512,512]{2,1,0:T(8,128)} collective-permute-done((f32[8,512,512]{2,1,0:T(8,128)}, f32[8,512,512]{2,1,0:T(8,128)}, u32[]{:S(2)}, u32[]{:S(2)}) %collective-permute-start.1) | collective-permute-done | bytes 8388640 | tf_op jit(solution)/shard_map/ppermute | solution.py:13
  653.4 11.3 add.235
  667.1 360.2 %collective-permute-done.2 = f32[8,512,512]{2,1,0:T(8,128)} collective-permute-done((f32[8,512,512]{2,1,0:T(8,128)}, f32[8,512,512]{2,1,0:T(8,128)}, u32[]{:S(2)}, u32[]{:S(2)}) %collective-permute-start.2) | collective-permute-done | bytes 8388640 | tf_op jit(solution)/shard_map/ppermute | solution.py:13
  1027.3 11.5 subtract_convert_fusion
  1051.7 3.3 fusion.191
  1055.0 3.3 fusion.119
  1058.3 3.3 fusion.138
  1061.6 3.3 fusion.154
  1064.9 3.3 fusion.167
  1068.2 3.3 fusion.177
  1071.6 3.3 fusion.184
  1084.8 3.3 fusion.113
  1088.1 3.4 fusion.132
  1091.5 3.3 fusion.148
  1094.8 3.3 fusion.161
  1104.0 3.4 fusion.107
  1107.4 3.3 fusion.126
  1110.7 3.4 fusion.89
  1114.1 4.5 bitcast_dynamic-update-slice_fusion.7
  1118.6 7.3 bitcast_dynamic-update-slice_fusion.6
  1125.9 3.6 bitcast_dynamic-update-slice_fusion.5
  1130.4 3.6 bitcast_dynamic-update-slice_fusion.4
  1134.1 3.5 bitcast_dynamic-update-slice_fusion.3
  1137.6 3.3 bitcast_dynamic-update-slice_fusion.2
  1140.9 3.3 bitcast_dynamic-update-slice_fusion.1
  1144.2 3.3 bitcast_dynamic-update-slice_fusion
  1147.6 154.8 %reduce-scatter.2.cloned.1.call-done = f32[8,128,1024]{2,1,0:T(8,128)} async-done(((f32[8,512,1024]{2,1,0:T(8,128)}), f32[8,128,1024]{2,1,0:T(8,128)}) %reduce-scatter.2.cloned.1.call-update) | async-done | bytes 4194320 | tf_op jit(solution)/shard_map/reduce_scatter | solution.py:88
  1302.4 4.6 multiply_convert_fusion
  1307.0 3.2 fusion.16
  1310.2 3.2 fusion.18
  1313.5 3.1 fusion.20
  1316.6 3.1 fusion.22
  1319.7 2.9 fusion.24
  1376.1 18.5 %all-gather.2.cloned.1.call-done = bf16[8,512,1024]{2,1,0:T(8,128)(2,1)} async-done(((bf16[8,128,1024]{2,1,0:T(8,128)(2,1)}), bf16[8,512,1024]{2,1,0:T(8,128)(2,1)}) %all-gather.2.cloned.1.call-update) | async-done | bytes 8388624 | tf_op jit(solution)/shard_map/all_gather | solution.py:90
  1394.6 10.5 convert_bitcast_fusion
  1405.1 11.4 copy.28
  1416.5 5.9 convert_reduce_fusion
  (141 shorter events, 130.8 us)
Async XLA Ops:
  7.2 325.6 %all-reduce.2.cloned.1.call-start = ((), (), s32[]{:S(2)}) async-start(), calls=%async_computation.1 | async-start | bytes 33554432 | tf_op jit(solution)/shard_map/psum | solution.py:39
  22.6 1.2 copy-start.11
  22.6 1279.8 %reduce-scatter.2.cloned.1.call-start = ((), (), s32[]{:S(2)}) async-start(), calls=%async_computation.2 | async-start | bytes 20971520 | tf_op jit(solution)/shard_map/reduce_scatter | solution.py:88
  24.3 308.5 %copy-start.12 = (f32[8,1024]{1,0:T(8,128)S(1)}, f32[8,1024]{1,0:T(8,128)}, u32[]{:S(2)}) copy-start(f32[8,1024]{1,0:T(8,128)} %param.9) | copy-start | bytes 98308
  332.8 39.1 %slice-start = ((s8[37748736]{0:T(1024)(128)(4,1)}), s8[4194304]{0:T(1024)(128)(4,1)S(1)}, s32[]{:S(2)}) async-start(s8[37748736]{0:T(1024)(128)(4,1)} %bitcast.586), calls=%async_computation.4 | async-start | bytes 8388608
  332.8 39.1 %slice-start.1 = ((s8[37748736]{0:T(1024)(128)(4,1)}), s8[4194304]{0:T(1024)(128)(4,1)S(1)}, s32[]{:S(2)}) async-start(s8[37748736]{0:T(1024)(128)(4,1)} %bitcast.586), calls=%async_computation.5 | async-start | bytes 8388608
  332.8 39.1 %slice-start.2 = ((s8[37748736]{0:T(1024)(128)(4,1)}), s8[4194304]{0:T(1024)(128)(4,1)S(1)}, s32[]{:S(2)}) async-start(s8[37748736]{0:T(1024)(128)(4,1)} %bitcast.586), calls=%async_computation.6 | async-start | bytes 8388608
  332.8 39.1 %slice-start.3 = ((s8[37748736]{0:T(1024)(128)(4,1)}), s8[4194304]{0:T(1024)(128)(4,1)S(1)}, s32[]{:S(2)}) async-start(s8[37748736]{0:T(1024)(128)(4,1)} %bitcast.586), calls=%async_computation.7 | async-start | bytes 8388608
  342.4 16.0 %copy-start.10 = (bf16[8,512,1024]{2,1,0:T(8,128)(2,1)}, bf16[8,512,1024]{2,1,0:T(8,128)(2,1)S(1)}, u32[]{:S(2)}) copy-start(bf16[8,512,1024]{2,1,0:T(8,128)(2,1)S(1)} %select_convert_fusion) | copy-start | bytes 25165828
  342.4 29.5 %slice-start.4 = ((s8[37748736]{0:T(1024)(128)(4,1)}), s8[4194304]{0:T(1024)(128)(4,1)S(1)}, s32[]{:S(2)}) async-start(s8[37748736]{0:T(1024)(128)(4,1)} %bitcast.586), calls=%async_computation.8 | async-start | bytes 8388608
  350.3 21.7 %slice-start.5 = ((s8[37748736]{0:T(1024)(128)(4,1)}), s8[4194304]{0:T(1024)(128)(4,1)S(1)}, s32[]{:S(2)}) async-start(s8[37748736]{0:T(1024)(128)(4,1)} %bitcast.586), calls=%async_computation.9 | async-start | bytes 8388608
  356.3 15.7 %slice-start.6 = ((s8[37748736]{0:T(1024)(128)(4,1)}), s8[4194304]{0:T(1024)(128)(4,1)S(1)}, s32[]{:S(2)}) async-start(s8[37748736]{0:T(1024)(128)(4,1)} %bitcast.586), calls=%async_computation.10 | async-start | bytes 8388608
  360.3 11.7 slice-start.7
  366.0 6.0 slice-start.8
  425.0 9.9 copy-start.14
  428.0 8.8 copy-start.13
  442.7 3.4 copy-start.2
  446.1 13.3 collective-permute-start
  470.6 182.8 %collective-permute-start.1 = (f32[8,512,512]{2,1,0:T(8,128)}, f32[8,512,512]{2,1,0:T(8,128)}, u32[]{:S(2)}, u32[]{:S(2)}) collective-permute-start(f32[8,512,512]{2,1,0:T(8,128)} %add.234), channel_id=1, source_target_pairs={{0,2},{1,3},{2,0},{3,1},{4,6},{5,7},{6,4},{7,5},{8,10},{9,11},{10,... | collective-permute-start | bytes 25165832 | tf_op jit(solution)/shard_map/ppermute | solution.py:13
  664.7 362.6 %collective-permute-start.2 = (f32[8,512,512]{2,1,0:T(8,128)}, f32[8,512,512]{2,1,0:T(8,128)}, u32[]{:S(2)}, u32[]{:S(2)}) collective-permute-start(f32[8,512,512]{2,1,0:T(8,128)} %add.235), channel_id=1, source_target_pairs={{0,4},{1,5},{2,6},{3,7},{4,0},{5,1},{6,2},{7,3},{8,12},{9,13},{10,... | collective-permute-start | bytes 25165832 | tf_op jit(solution)/shard_map/ppermute | solution.py:13
  1038.8 7.0 copy-start
  1125.9 3.7 copy-start.6
  1125.9 3.7 copy-start.7
  1125.9 3.7 copy-start.8
  1125.9 4.5 copy-start.9
  1130.4 7.1 copy-start.4
  1130.4 7.1 copy-start.5
  1134.1 6.8 copy-start.3
  1147.5 247.1 %all-gather.2.cloned.1.call-start = ((), (), s32[]{:S(2)}) async-start(), calls=%async_computation.3 | async-start | bytes 10485760 | tf_op jit(solution)/shard_map/all_gather | solution.py:90
  1307.0 6.5 copy-start.1
  1310.2 12.4 slice-start.9
  1316.6 6.1 slice-start.10
Sparse Core Ops, SparseCore 0:
  22.7 310.0 all-reduce.1
  1147.6 154.7 reduce-scatter.1
  1307.1 87.4 all-gather.1
